TPU v7x, 32 devices: a whole 2x2x4 slice. The times are simulated.
32 devices in a mesh: dp: 4 (over x, core), seq: 8 (over z, y).
Axes of the slice: x: 2, y: 2, z: 4, core: 2. Of those that a mesh axis runs over, the one named last changes fastest.
Arguments:
- q_raw: bfloat16 [4, 1024, 4096], P('dp', 'seq'), may hold values from -64 to 64
- k_raw: bfloat16 [4, 1024, 4096], P('dp', 'seq'), may hold values from -64 to 64
- values: bfloat16 [4, 1024, 4096], P('dp', 'seq'), may hold values from -6 to 6
- grad_out: bfloat16 [4, 1024, 4096], P('dp', 'seq'), may hold values from -6 to 6
- q_gain: float32 [4096], replicated, may hold values from 0.1 to 1.9
- k_gain: float32 [4096], replicated, may hold values from 0.1 to 1.9
- lengths: int32 [4, 6], P('dp'), may hold values from 1 to 341, 1024 in all within a row
- positions: int32 [4, 3, 1024], P('dp', None, 'seq'), may hold values from 0 to 63
Outputs:
- attended: bfloat16 [4, 1024, 4096], P('dp', 'seq')
- grad_q: bfloat16 [4, 1024, 4096], P('dp', 'seq')
- grad_k: bfloat16 [4, 1024, 4096], P('dp', 'seq')
- grad_v: bfloat16 [4, 1024, 4096], P('dp', 'seq')
- grad_q_gain: float32 [4096], replicated
- grad_k_gain: float32 [4096], replicated
Inputs may be any that keep to these rules, and one draw needn't show every extreme that they name: `lengths`: the clips of a bucket lie end to end and fill its 1024 tokens.
All inputs are finite; a program needn't handle non-finite values.
Results may differ from a plain program's by a relative error of at most 0.012.
The roundings to bfloat16 on the way count: a program that leaves them out, or rounds other values in their place, can miss the bound.
Values may be sent and summed in bfloat16 or wider, within the bound.
A program may use at most 128 MiB of HBM per device.

v0:
```python
import jax
import jax.numpy as jnp
from jax import lax
from jax.sharding import PartitionSpec as P

HEAD_DIM = 128
epsilon = 1e-06


def product(form, left, right):
    return jnp.einsum(form, left, right, preferred_element_type=jnp.float32)


def segment_ids(clip_lengths, tokens):
    boundary = jnp.cumsum(clip_lengths)
    places = jnp.arange(tokens, dtype=jnp.int32)
    return jnp.sum((boundary[None, :] <= places[:, None]).astype(jnp.int32), axis=1)


def rope_tables(position_rows, head_dim):
    half = head_dim // 2
    sixth = head_dim // 6
    first = half - 2 * sixth
    pairs = jnp.arange(half, dtype=jnp.int32)
    section = (pairs >= first).astype(jnp.int32) + (pairs >= first + sixth).astype(jnp.int32)
    begin = jnp.where(section == 0, 0, jnp.where(section == 1, first, first + sixth))
    number = jnp.where(section == 0, first, sixth)
    freqs = 10000.0 ** (-(pairs - begin).astype(jnp.float32) / number.astype(jnp.float32))
    picker = (section[None, :] == jnp.arange(3, dtype=jnp.int32)[:, None]).astype(
        jnp.float32
    ) * freqs[None, :]
    angle = lax.dot_general(
        position_rows.astype(jnp.float32),
        picker,
        (((0,), (0,)), ((), ())),
        precision=lax.Precision.HIGHEST,
    )
    cosine = jnp.cos(angle)
    sine = jnp.sin(angle)
    return (jnp.concatenate([cosine, cosine], axis=-1), jnp.concatenate([sine, sine], axis=-1))


def rotate_pairs(inputs, cosine, sine):
    half = inputs.shape[-1] // 2
    partner = jnp.concatenate([-inputs[..., half:], inputs[..., :half]], axis=-1)
    return inputs * cosine[:, None, :] + partner * sine[:, None, :]


def rotate_back(grads, cosine, sine):
    half = grads.shape[-1] // 2
    turned = grads * sine[:, None, :]
    return grads * cosine[:, None, :] + jnp.concatenate(
        [turned[..., half:], -turned[..., :half]], axis=-1
    )


def attention_forward(query, keys, value_rows, segment, block, window, reach):
    count = query.shape[0]
    scale = query.shape[2] ** (-0.5)

    def one_block(index_block):
        start = index_block * block
        key_start = jnp.clip(start - reach, 0, count - window)
        query_block = lax.dynamic_slice_in_dim(query, start, block, 0)
        key_window = lax.dynamic_slice_in_dim(keys, key_start, window, 0)
        value_window = lax.dynamic_slice_in_dim(value_rows, key_start, window, 0)
        query_clip = lax.dynamic_slice_in_dim(segment, start, block, 0)
        key_clip = lax.dynamic_slice_in_dim(segment, key_start, window, 0)
        scores = product("qhd,khd->hqk", query_block, key_window) * scale
        live = (query_clip[:, None] == key_clip[None, :])[None]
        scores = jnp.where(live, scores, -1e30)
        highest = jnp.max(scores, axis=-1, keepdims=True)
        expon = jnp.exp(scores - highest)
        totals = jnp.sum(expon, axis=-1, keepdims=True)
        weights = (expon / totals).astype(jnp.bfloat16)
        output = product("hqk,khd->qhd", weights, value_window)
        return (output, (highest + jnp.log(totals))[..., 0])

    outputs, logsum = lax.map(one_block, jnp.arange(count // block, dtype=jnp.int32))
    return (outputs.reshape(query.shape), logsum)


def attention_backward(
    query, keys, value_rows, context, cotangent, logsum, segment, block, window, reach
):
    count = query.shape[0]
    scale = query.shape[2] ** (-0.5)
    delta = jnp.sum(cotangent.astype(jnp.float32) * context.astype(jnp.float32), axis=-1)

    def one_block(carry, inputs):
        key_acc, value_acc = carry
        index_block, block_logsum = inputs
        start = index_block * block
        key_start = jnp.clip(start - reach, 0, count - window)
        query_block = lax.dynamic_slice_in_dim(query, start, block, 0)
        cot_block = lax.dynamic_slice_in_dim(cotangent, start, block, 0)
        delta_block = lax.dynamic_slice_in_dim(delta, start, block, 0)
        key_window = lax.dynamic_slice_in_dim(keys, key_start, window, 0)
        value_window = lax.dynamic_slice_in_dim(value_rows, key_start, window, 0)
        query_clip = lax.dynamic_slice_in_dim(segment, start, block, 0)
        key_clip = lax.dynamic_slice_in_dim(segment, key_start, window, 0)
        scores = product("qhd,khd->hqk", query_block, key_window) * scale
        live = (query_clip[:, None] == key_clip[None, :])[None]
        probs = jnp.where(live, jnp.exp(scores - block_logsum[:, :, None]), 0.0)
        prob_half = probs.astype(jnp.bfloat16)
        value_grad = product("hqk,qhd->khd", prob_half, cot_block)
        dprob = product("qhd,khd->hqk", cot_block, value_window)
        dscore = (probs * (dprob - jnp.transpose(delta_block)[:, :, None]) * scale).astype(
            jnp.bfloat16
        )
        query_grad = product("hqk,khd->qhd", dscore, key_window)
        key_grad = product("hqk,qhd->khd", dscore, query_block)
        key_acc = lax.dynamic_update_slice_in_dim(
            key_acc,
            lax.dynamic_slice_in_dim(key_acc, key_start, window, 0) + key_grad,
            key_start,
            0,
        )
        value_acc = lax.dynamic_update_slice_in_dim(
            value_acc,
            lax.dynamic_slice_in_dim(value_acc, key_start, window, 0) + value_grad,
            key_start,
            0,
        )
        return ((key_acc, value_acc), query_grad)

    zeros = jnp.zeros(query.shape, jnp.float32)
    indices = jnp.arange(count // block, dtype=jnp.int32)
    (key_acc, value_acc), query_grads = lax.scan(one_block, (zeros, zeros), (indices, logsum))
    return (query_grads.reshape(query.shape), key_acc, value_acc)


def on_device(q_raw, k_raw, values, grad_out, q_gain, k_gain, lengths, positions):
    members = lax.axis_size("seq")
    replicas = lax.axis_size("dp")
    tok_dev = q_raw.shape[1]
    feature = q_raw.shape[2]
    tokens = tok_dev * members
    share = feature // members
    local_heads = share // HEAD_DIM
    reach = tokens // 3
    block = min(512, tokens)
    window = min(tokens, block + 2 * reach)
    segment = segment_ids(lengths[0], tokens)
    cosine, sine = rope_tables(positions[0], HEAD_DIM)
    query_float = q_raw[0].astype(jnp.float32)
    key_float = k_raw[0].astype(jnp.float32)
    query_scale = lax.rsqrt(jnp.mean(query_float * query_float, axis=-1) + epsilon)
    key_scale = lax.rsqrt(jnp.mean(key_float * key_float, axis=-1) + epsilon)
    query_hat = query_float * query_scale[:, None]
    key_hat = key_float * key_scale[:, None]
    query_rot = rotate_pairs((query_hat * q_gain).reshape(tok_dev, -1, HEAD_DIM), cosine, sine)
    key_rot = rotate_pairs((key_hat * k_gain).reshape(tok_dev, -1, HEAD_DIM), cosine, sine)
    sent = (
        query_rot.astype(jnp.bfloat16).reshape(1, tok_dev, feature),
        key_rot.astype(jnp.bfloat16).reshape(1, tok_dev, feature),
        values,
    )
    got_query, got_key, got_value = (
        lax.all_to_all(sent[0], "seq", split_axis=2, concat_axis=1, tiled=True),
        lax.all_to_all(sent[1], "seq", split_axis=2, concat_axis=1, tiled=True),
        lax.all_to_all(sent[2], "seq", split_axis=2, concat_axis=1, tiled=True),
    )
    query_heads = got_query[0].reshape(tokens, local_heads, HEAD_DIM)
    key_heads = got_key[0].reshape(tokens, local_heads, HEAD_DIM)
    value_heads = got_value[0].reshape(tokens, local_heads, HEAD_DIM)
    context, logsum = attention_forward(
        query_heads, key_heads, value_heads, segment, block, window, reach
    )
    context_half = context.astype(jnp.bfloat16)
    attended = lax.all_to_all(
        context_half.reshape(1, tokens, share), "seq", split_axis=1, concat_axis=2, tiled=True
    )
    cotangent = lax.all_to_all(grad_out, "seq", split_axis=2, concat_axis=1, tiled=True)[0].reshape(
        tokens, local_heads, HEAD_DIM
    )
    query_grad, key_grad, value_grad = attention_backward(
        query_heads,
        key_heads,
        value_heads,
        context_half,
        cotangent,
        logsum,
        segment,
        block,
        window,
        reach,
    )
    query_half = query_grad.astype(jnp.bfloat16)
    key_half = key_grad.astype(jnp.bfloat16)
    value_half = value_grad.astype(jnp.bfloat16).reshape(1, tokens, share)
    sent_back = (
        query_half.reshape(1, tokens, share),
        key_half.reshape(1, tokens, share),
        value_half,
    )
    back_query, back_key, back_value = (
        lax.all_to_all(sent_back[0], "seq", split_axis=1, concat_axis=2, tiled=True),
        lax.all_to_all(sent_back[1], "seq", split_axis=1, concat_axis=2, tiled=True),
        lax.all_to_all(sent_back[2], "seq", split_axis=1, concat_axis=2, tiled=True),
    )
    query_back = rotate_back(
        back_query[0].astype(jnp.float32).reshape(tok_dev, -1, HEAD_DIM), cosine, sine
    ).reshape(tok_dev, feature)
    key_back = rotate_back(
        back_key[0].astype(jnp.float32).reshape(tok_dev, -1, HEAD_DIM), cosine, sine
    ).reshape(tok_dev, feature)
    query_part = jnp.sum(query_back * query_hat, axis=0)
    key_part = jnp.sum(key_back * key_hat, axis=0)
    query_lift = query_back * q_gain
    key_lift = key_back * k_gain
    query_input = query_scale[:, None] * (
        query_lift - query_hat * jnp.mean(query_lift * query_hat, axis=-1, keepdims=True)
    )
    key_input = key_scale[:, None] * (
        key_lift - key_hat * jnp.mean(key_lift * key_hat, axis=-1, keepdims=True)
    )
    gains = lax.psum(jnp.stack([query_part, key_part]), ("dp", "seq")) / replicas
    grad_query_input = query_input.astype(jnp.bfloat16)[None]
    grad_key_input = key_input.astype(jnp.bfloat16)[None]
    return (attended, grad_query_input, grad_key_input, back_value, gains[0], gains[1])


def solution(mesh):
    return jax.shard_map(
        on_device,
        mesh=mesh,
        in_specs=(
            P("dp", "seq", None),
            P("dp", "seq", None),
            P("dp", "seq", None),
            P("dp", "seq", None),
            P(),
            P(),
            P("dp", None),
            P("dp", None, "seq"),
        ),
        out_specs=(
            P("dp", "seq", None),
            P("dp", "seq", None),
            P("dp", "seq", None),
            P("dp", "seq", None),
            P(),
            P(),
        ),
        check_vma=False,
    )
```

profile of v0, /device:TPU:0, one launch (start us, length us, event | category | flops | bytes accessed | tf_op | source)
XLA Modules:
  0.0 501.7 jit_solution(1113454433465873790)
XLA Ops:
  12.2 16.7 %copy.213 = bf16[1,128,4096]{1,0,2:T(2,128)(2,1)S(1)} copy(bf16[1,128,4096]{1,2,0:T(8,128)(2,1)S(1)} %get-tuple-element.342) | data formatting | bytes 2097152 | tf_op jit(solution)/shard_map/convert_element_type | solution.py:155
  29.4 23.4 %reduce.10 = bf16[4096,128]{1,0:T(8,128)(2,1)} reduce(bf16[4096,1,128]{2,1,0:T(2,128)(2,1)S(1)} %bitcast.238, bf16[]{:T(256)} %broadcast.330), dimensions={1}, to_apply=%bitcast.188.reduce_sub_computation | reduce | bytes 2097154
  54.9 7.5 %all-to-all-start = ((bf16[8,2,32768]{2,1,0:T(2,128)(2,1)}), bf16[8,2,32768]{2,1,0:T(2,128)(2,1)}, u32[]{:S(2)}, u32[]{:S(2)}) async-start(bf16[8,2,32768]{2,1,0:T(2,128)(2,1)} %reshape.589), calls=%async_computation | async-start | bytes 2097152 | tf_op jit(solution)/shard_map/all_to_all | solution.py:160
  62.5 16.7 %copy.212 = bf16[1,128,4096]{1,0,2:T(2,128)(2,1)S(1)} copy(bf16[1,128,4096]{1,2,0:T(8,128)(2,1)S(1)} %get-tuple-element.341) | data formatting | bytes 2097152 | tf_op jit(solution)/shard_map/convert_element_type | solution.py:156
  79.2 22.4 %reduce.11 = bf16[4096,128]{1,0:T(8,128)(2,1)S(1)} reduce(bf16[4096,1,128]{2,1,0:T(2,128)(2,1)S(1)} %bitcast.241, bf16[]{:T(256)} %broadcast.330), dimensions={1}, to_apply=%bitcast.187.reduce_sub_computation | reduce | bytes 2097154
  102.7 6.0 %all-to-all-start.1 = ((bf16[8,2,32768]{2,1,0:T(2,128)(2,1)}), bf16[8,2,32768]{2,1,0:T(2,128)(2,1)S(1)}, u32[]{:S(2)}, u32[]{:S(2)}) async-start(bf16[8,2,32768]{2,1,0:T(2,128)(2,1)} %reshape.591), calls=%async_computation.1 | async-start | bytes 2097152 | tf_op jit(solution)/shard_map/all_to_all | solution.py:161
  113.8 23.4 %reduce.12 = bf16[4096,128]{1,0:T(8,128)(2,1)} reduce(bf16[4096,1,128]{2,1,0:T(2,128)(2,1)S(1)} %bitcast.245, bf16[]{:T(256)} %broadcast.330), dimensions={1}, to_apply=%bitcast.164.reduce_sub_computation | reduce | bytes 2097154
  139.3 6.3 %all-to-all-start.2 = ((bf16[8,2,32768]{2,1,0:T(2,128)(2,1)}), bf16[8,2,32768]{2,1,0:T(2,128)(2,1)}, u32[]{:S(2)}, u32[]{:S(2)}) async-start(bf16[8,2,32768]{2,1,0:T(2,128)(2,1)} %reshape.593), calls=%async_computation.2 | async-start | bytes 2097152 | tf_op jit(solution)/shard_map/all_to_all | solution.py:162
  145.8 5.5 %copy.167 = bf16[1,128,4096]{1,0,2:T(2,128)(2,1)} copy(bf16[1,128,4096]{2,1,0:T(8,128)(2,1)} %param.15) | data formatting | bytes 2097152 | tf_op args[3]
  151.3 24.4 %reduce.14 = bf16[4096,128]{1,0:T(8,128)(2,1)} reduce(bf16[4096,1,128]{2,1,0:T(2,128)(2,1)} %bitcast.246, bf16[]{:T(256)} %broadcast.330), dimensions={1}, to_apply=%bitcast.168.reduce_sub_computation | reduce | bytes 2097154
  177.9 5.8 %reshape.590 = bf16[4096,1,128]{2,1,0:T(2,128)(2,1)} reshape(bf16[8,2,32768]{2,1,0:T(2,128)(2,1)} %all-to-all-done) | data formatting | bytes 2097152
  200.4 6.5 %all-to-all-start.4 = ((bf16[8,2,32768]{2,1,0:T(2,128)(2,1)}), bf16[8,2,32768]{2,1,0:T(2,128)(2,1)}, u32[]{:S(2)}, u32[]{:S(2)}) async-start(bf16[8,2,32768]{2,1,0:T(2,128)(2,1)} %reshape.597), calls=%async_computation.4 | async-start | bytes 2097152 | tf_op jit(solution)/shard_map/all_to_all | solution.py:174
  206.8 5.8 %reshape.594 = bf16[4096,1,128]{2,1,0:T(2,128)(2,1)} reshape(bf16[8,2,32768]{2,1,0:T(2,128)(2,1)} %all-to-all-done.2) | data formatting | bytes 2097152
  221.7 21.2 %while.27 = (s32[]{:T(128)}, bf16[2,512,4,128]{3,1,2,0:T(8,128)(2,1)}, f32[2,4,512]{2,1,0:T(4,128)S(1)}, s32[2]{0:T(128)S(1)}, s32[1024]{0:T(1024)S(1)}, /*index...) while((s32[]{:T(128)}, ...), condition=%wide.region_7.8_spmd, body=%wide.region_4.7_spmd.sunk | while | flops 1099429888 | bytes 35203796 | solution.py:79
  250.7 5.8 %reshape.598 = bf16[4096,1,128]{2,1,0:T(2,128)(2,1)} reshape(bf16[8,2,32768]{2,1,0:T(2,128)(2,1)} %all-to-all-done.4) | data formatting | bytes 2097152
  265.4 47.3 %while.28 = (s32[]{:T(128)}, f32[1024,4,128]{0,2,1:T(8,128)S(1)}, f32[1024,4,128]{0,2,1:T(8,128)}, bf16[2,512,4,128]{3,1,2,0:T(8,128)(2,1)}, s32[2]{0:T(128)S(1)...) while((s32[]{:T(128)}, f32[1024,4,128]{0,2,1:T(8,128)S(1)}, ...), condition=%wide.region_10.11_spmd.clone, body=%wide.region_9.10_spmd.clone.sunk | while | flops 2710044672 | bytes 154733552 | solution.py:129
  318.1 8.0 %reduce.16 = bf16[1024,512]{1,0:T(8,128)(2,1)S(1)} reduce(bf16[1024,1,512]{2,1,0:T(2,128)(2,1)} %bitcast.242, bf16[]{:T(256)} %broadcast.330), dimensions={1}, to_apply=%bitcast.170.reduce_sub_computation | reduce | bytes 2097154
  327.7 6.3 %all-to-all-start.5 = ((bf16[8,2,32768]{2,1,0:T(2,128)(2,1)}), bf16[8,2,32768]{2,1,0:T(2,128)(2,1)}, u32[]{:S(2)}, u32[]{:S(2)}) async-start(bf16[8,2,32768]{2,1,0:T(2,128)(2,1)} %reshape.599), calls=%async_computation.5 | async-start | bytes 2097152 | tf_op jit(solution)/shard_map/all_to_all | solution.py:198
  336.1 7.0 %reduce.15 = bf16[1024,512]{1,0:T(8,128)(2,1)S(1)} reduce(bf16[1024,1,512]{2,1,0:T(2,128)(2,1)S(1)} %bitcast.243, bf16[]{:T(256)} %broadcast.330), dimensions={1}, to_apply=%bitcast.172.reduce_sub_computation | reduce | bytes 2097154
  344.7 13.1 %all-to-all-done.5 = bf16[8,2,32768]{2,1,0:T(2,128)(2,1)} async-done(((bf16[8,2,32768]{2,1,0:T(2,128)(2,1)}), bf16[8,2,32768]{2,1,0:T(2,128)(2,1)}, u32[]{:S(2)}, u32[]{:S(2)}) %all-to-all-start.5) | async-done | bytes 1048608 | tf_op jit(solution)/shard_map/all_to_all | solution.py:198
  374.3 8.1 %reduce.17 = bf16[1024,512]{1,0:T(8,128)(2,1)} reduce(bf16[1024,1,512]{2,1,0:T(2,128)(2,1)S(1)} %bitcast.244, bf16[]{:T(256)} %broadcast.330), dimensions={1}, to_apply=%bitcast.174.reduce_sub_computation | reduce | bytes 2097154
  385.7 7.0 %reduce.13 = bf16[1024,512]{1,0:T(8,128)(2,1)S(1)} reduce(bf16[1024,1,512]{2,1,0:T(2,128)(2,1)S(1)} %bitcast.240, bf16[]{:T(256)} %broadcast.330), dimensions={1}, to_apply=%bitcast.166.reduce_sub_computation | reduce | bytes 2097154
  403.6 6.0 %all-to-all-start.7 = ((bf16[8,2,32768]{2,1,0:T(2,128)(2,1)}), bf16[8,2,32768]{2,1,0:T(2,128)(2,1)}, u32[]{:S(2)}, u32[]{:S(2)}) async-start(bf16[8,2,32768]{2,1,0:T(2,128)(2,1)} %reshape.603), calls=%async_computation.7 | async-start | bytes 2097152 | tf_op jit(solution)/shard_map/all_to_all | solution.py:200
  453.4 40.8 %psum.7 = f32[2,4096]{1,0:T(2,128)S(1)} all-reduce(f32[2,4096]{1,0:T(2,128)S(1)} %pad_maximum_fusion.4), channel_id=1, replica_groups=mesh['dp'=4,'seq'=8] {'dp','seq'}, use_global_device_ids=true, to_apply=%region_15.16 | all-reduce | flops 8192 | bytes 65536 | tf_op jit(solution)/shard_map/psum | solution.py:218
  (236 shorter events, 224.5 us)
Async XLA Ops:
  2.3 8.3 %copy-start.3 = (bf16[1,128,4096]{1,2,0:T(8,128)(2,1)}, bf16[1,128,4096]{1,2,0:T(8,128)(2,1)S(1)}, u32[]{:S(2)}) copy-start(bf16[1,128,4096]{1,2,0:T(8,128)(2,1)S(1)} %copy.156) | copy-start | bytes 3145732
  5.0 5.6 %copy-start.5 = (bf16[1,128,4096]{1,2,0:T(8,128)(2,1)}, bf16[1,128,4096]{1,2,0:T(8,128)(2,1)S(1)}, u32[]{:S(2)}) copy-start(bf16[1,128,4096]{1,2,0:T(8,128)(2,1)S(1)} %copy.153) | copy-start | bytes 3145732
  5.8 4.8 copy-start.31
  5.8 4.8 copy-start.33
  54.9 47.8 %all-to-all-start = ((bf16[8,2,32768]{2,1,0:T(2,128)(2,1)}), bf16[8,2,32768]{2,1,0:T(2,128)(2,1)}, u32[]{:S(2)}, u32[]{:S(2)}) async-start(bf16[8,2,32768]{2,1,0:T(2,128)(2,1)} %reshape.589), calls=%async_computation | async-start | bytes 2097152 | tf_op jit(solution)/shard_map/all_to_all | solution.py:160
  102.7 36.5 %all-to-all-start.1 = ((bf16[8,2,32768]{2,1,0:T(2,128)(2,1)}), bf16[8,2,32768]{2,1,0:T(2,128)(2,1)S(1)}, u32[]{:S(2)}, u32[]{:S(2)}) async-start(bf16[8,2,32768]{2,1,0:T(2,128)(2,1)} %reshape.591), calls=%async_computation.1 | async-start | bytes 2097152 | tf_op jit(solution)/shard_map/all_to_all | solution.py:161
  137.1 8.4 %copy-start.36 = (s32[1,6]{1,0:T(1,128)S(1)}, s32[1,6]{1,0:T(1,128)}, u32[]{:S(2)}) copy-start(s32[1,6]{1,0:T(1,128)} %param.18) | copy-start | bytes 76
  139.3 61.1 %all-to-all-start.2 = ((bf16[8,2,32768]{2,1,0:T(2,128)(2,1)}), bf16[8,2,32768]{2,1,0:T(2,128)(2,1)}, u32[]{:S(2)}, u32[]{:S(2)}) async-start(bf16[8,2,32768]{2,1,0:T(2,128)(2,1)} %reshape.593), calls=%async_computation.2 | async-start | bytes 2097152 | tf_op jit(solution)/shard_map/all_to_all | solution.py:162
  200.4 50.3 %all-to-all-start.4 = ((bf16[8,2,32768]{2,1,0:T(2,128)(2,1)}), bf16[8,2,32768]{2,1,0:T(2,128)(2,1)}, u32[]{:S(2)}, u32[]{:S(2)}) async-start(bf16[8,2,32768]{2,1,0:T(2,128)(2,1)} %reshape.597), calls=%async_computation.4 | async-start | bytes 2097152 | tf_op jit(solution)/shard_map/all_to_all | solution.py:174
  266.8 5.9 %copy-start.15 = (bf16[1024,4,128]{0,2,1:T(8,128)(2,1)S(1)}, bf16[1024,4,128]{0,2,1:T(8,128)(2,1)}, u32[]{:S(2)}) copy-start(bf16[1024,4,128]{0,2,1:T(8,128)(2,1)} %get-tuple-element.556) | copy-start | bytes 3145732 | tf_op jit(solution)/shard_map/while
  266.9 5.9 %copy-start.24 = (bf16[1024,4,128]{2,0,1:T(8,128)(2,1)S(1)}, bf16[1024,4,128]{2,0,1:T(8,128)(2,1)}, u32[]{:S(2)}) copy-start(bf16[1024,4,128]{2,0,1:T(8,128)(2,1)} %get-tuple-element.557) | copy-start | bytes 3145732 | tf_op jit(solution)/shard_map/while
  277.8 6.2 %copy-start.2 = (f32[4,512,1024]{2,1,0:T(8,128)S(1)}, f32[4,512,1024]{2,1,0:T(8,128)}, u32[]{:S(2)}) copy-start(f32[4,512,1024]{2,1,0:T(8,128)} %copy-done.1) | copy-start | bytes 25165828 | tf_op jit(solution)/shard_map/while
  289.8 5.9 %copy-start.15 = (bf16[1024,4,128]{0,2,1:T(8,128)(2,1)S(1)}, bf16[1024,4,128]{0,2,1:T(8,128)(2,1)}, u32[]{:S(2)}) copy-start(bf16[1024,4,128]{0,2,1:T(8,128)(2,1)} %get-tuple-element.556) | copy-start | bytes 3145732 | tf_op jit(solution)/shard_map/while
  289.8 5.9 %copy-start.24 = (bf16[1024,4,128]{2,0,1:T(8,128)(2,1)S(1)}, bf16[1024,4,128]{2,0,1:T(8,128)(2,1)}, u32[]{:S(2)}) copy-start(bf16[1024,4,128]{2,0,1:T(8,128)(2,1)} %get-tuple-element.557) | copy-start | bytes 3145732 | tf_op jit(solution)/shard_map/while
  300.8 6.2 %copy-start.2 = (f32[4,512,1024]{2,1,0:T(8,128)S(1)}, f32[4,512,1024]{2,1,0:T(8,128)}, u32[]{:S(2)}) copy-start(f32[4,512,1024]{2,1,0:T(8,128)} %copy-done.1) | copy-start | bytes 25165828 | tf_op jit(solution)/shard_map/while
  327.7 30.1 %all-to-all-start.5 = ((bf16[8,2,32768]{2,1,0:T(2,128)(2,1)}), bf16[8,2,32768]{2,1,0:T(2,128)(2,1)}, u32[]{:S(2)}, u32[]{:S(2)}) async-start(bf16[8,2,32768]{2,1,0:T(2,128)(2,1)} %reshape.599), calls=%async_computation.5 | async-start | bytes 2097152 | tf_op jit(solution)/shard_map/all_to_all | solution.py:198
  343.1 19.4 %copy-start.30 = (f32[4096]{0:T(1024)S(1)}, f32[4096]{0:T(1024)}, u32[]{:S(2)}) copy-start(f32[4096]{0:T(1024)} %param.16) | copy-start | bytes 49156
  343.1 19.4 %copy-start.28 = (f32[4096]{0:T(1024)S(1)}, f32[4096]{0:T(1024)}, u32[]{:S(2)}) copy-start(f32[4096]{0:T(1024)} %param.17) | copy-start | bytes 49156
  343.1 19.5 %copy-start.21 = (f32[128,128]{0,1:T(8,128)S(1)}, f32[128,128]{0,1:T(8,128)}, u32[]{:S(2)}) copy-start(f32[128,128]{0,1:T(8,128)} %copy-done.20) | copy-start | bytes 196612
  357.8 45.8 %all-to-all-start.6 = ((bf16[8,2,32768]{2,1,0:T(2,128)(2,1)}), bf16[8,2,32768]{2,1,0:T(2,128)(2,1)}, u32[]{:S(2)}, u32[]{:S(2)}) async-start(bf16[8,2,32768]{2,1,0:T(2,128)(2,1)} %reshape.601), calls=%async_computation.6 | async-start | bytes 2097152 | tf_op jit(solution)/shard_map/all_to_all | solution.py:199
  374.3 10.7 %copy-start.17 = (bf16[2,512,4,128]{3,2,1,0:T(4,128)(2,1)S(1)}, bf16[2,512,4,128]{3,2,1,0:T(4,128)(2,1)}, u32[]{:S(2)}) copy-start(bf16[2,512,4,128]{3,2,1,0:T(4,128)(2,1)} %copy.164) | copy-start | bytes 3145732
  403.6 30.2 %all-to-all-start.7 = ((bf16[8,2,32768]{2,1,0:T(2,128)(2,1)}), bf16[8,2,32768]{2,1,0:T(2,128)(2,1)}, u32[]{:S(2)}, u32[]{:S(2)}) async-start(bf16[8,2,32768]{2,1,0:T(2,128)(2,1)} %reshape.603), calls=%async_computation.7 | async-start | bytes 2097152 | tf_op jit(solution)/shard_map/all_to_all | solution.py:200
  431.4 6.9 %copy-start.4 = (bf16[1,128,4096]{1,2,0:T(8,128)(2,1)S(1)}, bf16[1,128,4096]{1,2,0:T(8,128)(2,1)}, u32[]{:S(2)}) copy-start(bf16[1,128,4096]{1,2,0:T(8,128)(2,1)} %copy-done.3) | copy-start | bytes 3145732
  433.8 61.0 %all-to-all-start.3 = ((bf16[8,2,32768]{2,1,0:T(2,128)(2,1)}), bf16[8,2,32768]{2,1,0:T(2,128)(2,1)}, u32[]{:S(2)}, u32[]{:S(2)}) async-start(bf16[8,2,32768]{2,1,0:T(2,128)(2,1)} %reshape.595), calls=%async_computation.3 | async-start | bytes 2097152 | tf_op jit(solution)/shard_map/all_to_all | solution.py:171
  (30 other events, 76.9 us)
where the time goes:
time: 511 us; the launch traced here: 502 us
  local copies, waits for them, and re-layouts  186 us (36%)
  other arithmetic  159 us (31%)
  matrix products  48.8 us (10%)
  starting transfers between devices  47.7 us (9%)
  blocking collectives  40.8 us (8%)
  waiting for transfers between devices  15.5 us (3%)
    unnamed x10, other arithmetic  124 us
    unnamed x89, local copies, waits for them, and re-layouts  85 us
    dot_general x14, matrix products, product(): return jnp.einsum(form, left, right, preferred_element_type=jnp.float32)  48.4 us
    psum x1, blocking collectives, on_device(): lax.psum(jnp.stack([query_part, key_part]), ('dp', 'seq')) / replicas  40.8 us
    convert_element_type x1, local copies, waits for them, and re-layouts, on_device(): query_rot.astype(jnp.bfloat16).reshape(1, tok_dev, feature)  16.7 us
    convert_element_type x1, local copies, waits for them, and re-layouts, on_device(): key_rot.astype(jnp.bfloat16).reshape(1, tok_dev, feature)  16.7 us
    all_to_all x1, waiting for transfers between devices, on_device(): lax.all_to_all(sent_back[0], 'seq', split_axis=1, concat_axis=2, tiled=True)  13.1 us
  transfers between devices with their start and end apart: 8, of which 2 were waited for; matrix products, arithmetic and copies ran while one was open for 51% of the time, Pallas kernels for 0%

commit v1 on v0

--- a/solution.py
+++ b/solution.py
@@ -215,7 +215,7 @@
     key_input = key_scale[:, None] * (
         key_lift - key_hat * jnp.mean(key_lift * key_hat, axis=-1, keepdims=True)
     )
-    gains = lax.psum(jnp.stack([query_part, key_part]), ("dp", "seq")) / replicas
+    gains = lax.psum(lax.psum(jnp.stack([query_part, key_part]), "seq"), "dp") / replicas
     grad_query_input = query_input.astype(jnp.bfloat16)[None]
     grad_key_input = key_input.astype(jnp.bfloat16)[None]
     return (attended, grad_query_input, grad_key_input, back_value, gains[0], gains[1])

time: 511 us -> 529 us (1.035)
  blocking collectives: 40.8 us -> 58.5 us
    psum x1 -> x2, blocking collectives: 40.8 us -> 58.5 us  [the longest x1 48.3 us: on_device(): lax.psum(jnp.stack([query_part, key_part]), 'seq')]
  transfers between devices with their start and end apart: 8 -> 8, of which waited for: 2 -> 2; matrix products, arithmetic and copies ran while one was open for 51% -> 49% of each run, Pallas kernels for 0% -> 0%
where the time goes in v1:
time: 529 us; the launch traced here: 519 us
  local copies, waits for them, and re-layouts  186 us (35%)
  other arithmetic  158 us (30%)
  blocking collectives  58.5 us (11%)
  matrix products  48.9 us (9%)
  starting transfers between devices  47.5 us (9%)
  waiting for transfers between devices  15.5 us (3%)
    unnamed x10, other arithmetic  124 us
    unnamed x89, local copies, waits for them, and re-layouts  85.1 us
    dot_general x14, matrix products, product(): return jnp.einsum(form, left, right, preferred_element_type=jnp.float32)  48.5 us
    psum x1, blocking collectives, on_device(): lax.psum(jnp.stack([query_part, key_part]), 'seq')  48.3 us
    convert_element_type x1, local copies, waits for them, and re-layouts, on_device(): query_rot.astype(jnp.bfloat16).reshape(1, tok_dev, feature)  16.7 us
    convert_element_type x1, local copies, waits for them, and re-layouts, on_device(): key_rot.astype(jnp.bfloat16).reshape(1, tok_dev, feature)  16.7 us
    all_to_all x1, waiting for transfers between devices, on_device(): lax.all_to_all(sent_back[0], 'seq', split_axis=1, concat_axis=2, tiled=True)  13.1 us
  transfers between devices with their start and end apart: 8, of which 2 were waited for; matrix products, arithmetic and copies ran while one was open for 49% of the time, Pallas kernels for 0%

profile of v1, /device:TPU:0, one launch (start us, length us, event | category | flops | bytes accessed | tf_op | source)
XLA Modules:
  0.0 519.3 jit_solution(11859626062586112865)
XLA Ops:
  12.2 16.7 %copy.213 = bf16[1,128,4096]{1,0,2:T(2,128)(2,1)S(1)} copy(bf16[1,128,4096]{1,2,0:T(8,128)(2,1)S(1)} %get-tuple-element.342) | data formatting | bytes 2097152 | tf_op jit(solution)/shard_map/convert_element_type | solution.py:155
  29.5 23.4 %reduce.10 = bf16[4096,128]{1,0:T(8,128)(2,1)} reduce(bf16[4096,1,128]{2,1,0:T(2,128)(2,1)S(1)} %bitcast.238, bf16[]{:T(256)} %broadcast.330), dimensions={1}, to_apply=%bitcast.188.reduce_sub_computation | reduce | bytes 2097154
  54.9 7.5 %all-to-all-start = ((bf16[8,2,32768]{2,1,0:T(2,128)(2,1)}), bf16[8,2,32768]{2,1,0:T(2,128)(2,1)}, u32[]{:S(2)}, u32[]{:S(2)}) async-start(bf16[8,2,32768]{2,1,0:T(2,128)(2,1)} %reshape.589), calls=%async_computation | async-start | bytes 2097152 | tf_op jit(solution)/shard_map/all_to_all | solution.py:160
  62.5 16.7 %copy.212 = bf16[1,128,4096]{1,0,2:T(2,128)(2,1)S(1)} copy(bf16[1,128,4096]{1,2,0:T(8,128)(2,1)S(1)} %get-tuple-element.341) | data formatting | bytes 2097152 | tf_op jit(solution)/shard_map/convert_element_type | solution.py:156
  79.2 22.4 %reduce.11 = bf16[4096,128]{1,0:T(8,128)(2,1)S(1)} reduce(bf16[4096,1,128]{2,1,0:T(2,128)(2,1)S(1)} %bitcast.241, bf16[]{:T(256)} %broadcast.330), dimensions={1}, to_apply=%bitcast.187.reduce_sub_computation | reduce | bytes 2097154
  102.7 6.0 %all-to-all-start.1 = ((bf16[8,2,32768]{2,1,0:T(2,128)(2,1)}), bf16[8,2,32768]{2,1,0:T(2,128)(2,1)S(1)}, u32[]{:S(2)}, u32[]{:S(2)}) async-start(bf16[8,2,32768]{2,1,0:T(2,128)(2,1)} %reshape.591), calls=%async_computation.1 | async-start | bytes 2097152 | tf_op jit(solution)/shard_map/all_to_all | solution.py:161
  113.8 23.4 %reduce.12 = bf16[4096,128]{1,0:T(8,128)(2,1)} reduce(bf16[4096,1,128]{2,1,0:T(2,128)(2,1)S(1)} %bitcast.245, bf16[]{:T(256)} %broadcast.330), dimensions={1}, to_apply=%bitcast.164.reduce_sub_computation | reduce | bytes 2097154
  139.3 6.3 %all-to-all-start.2 = ((bf16[8,2,32768]{2,1,0:T(2,128)(2,1)}), bf16[8,2,32768]{2,1,0:T(2,128)(2,1)}, u32[]{:S(2)}, u32[]{:S(2)}) async-start(bf16[8,2,32768]{2,1,0:T(2,128)(2,1)} %reshape.593), calls=%async_computation.2 | async-start | bytes 2097152 | tf_op jit(solution)/shard_map/all_to_all | solution.py:162
  151.3 24.4 %reduce.14 = bf16[4096,128]{1,0:T(8,128)(2,1)} reduce(bf16[4096,1,128]{2,1,0:T(2,128)(2,1)} %bitcast.246, bf16[]{:T(256)} %broadcast.330), dimensions={1}, to_apply=%bitcast.168.reduce_sub_computation | reduce | bytes 2097154
  177.9 5.8 %reshape.590 = bf16[4096,1,128]{2,1,0:T(2,128)(2,1)} reshape(bf16[8,2,32768]{2,1,0:T(2,128)(2,1)} %all-to-all-done) | data formatting | bytes 2097152
  200.4 6.5 %all-to-all-start.4 = ((bf16[8,2,32768]{2,1,0:T(2,128)(2,1)}), bf16[8,2,32768]{2,1,0:T(2,128)(2,1)}, u32[]{:S(2)}, u32[]{:S(2)}) async-start(bf16[8,2,32768]{2,1,0:T(2,128)(2,1)} %reshape.597), calls=%async_computation.4 | async-start | bytes 2097152 | tf_op jit(solution)/shard_map/all_to_all | solution.py:174
  206.9 5.8 %reshape.594 = bf16[4096,1,128]{2,1,0:T(2,128)(2,1)} reshape(bf16[8,2,32768]{2,1,0:T(2,128)(2,1)} %all-to-all-done.2) | data formatting | bytes 2097152
  221.7 21.2 %while.27 = (s32[]{:T(128)}, bf16[2,512,4,128]{3,1,2,0:T(8,128)(2,1)}, f32[2,4,512]{2,1,0:T(4,128)S(1)}, s32[2]{0:T(128)S(1)}, s32[1024]{0:T(1024)S(1)}, /*index...) while((s32[]{:T(128)}, ...), condition=%wide.region_7.8_spmd, body=%wide.region_4.7_spmd.sunk | while | flops 1099429888 | bytes 35203796 | solution.py:79
  250.7 5.8 %reshape.598 = bf16[4096,1,128]{2,1,0:T(2,128)(2,1)} reshape(bf16[8,2,32768]{2,1,0:T(2,128)(2,1)} %all-to-all-done.4) | data formatting | bytes 2097152
  265.5 47.4 %while.28 = (s32[]{:T(128)}, f32[1024,4,128]{0,2,1:T(8,128)S(1)}, f32[1024,4,128]{0,2,1:T(8,128)}, bf16[2,512,4,128]{3,1,2,0:T(8,128)(2,1)}, s32[2]{0:T(128)S(1)...) while((s32[]{:T(128)}, f32[1024,4,128]{0,2,1:T(8,128)S(1)}, ...), condition=%wide.region_10.11_spmd.clone, body=%wide.region_9.10_spmd.clone.sunk | while | flops 2710044672 | bytes 154733552 | solution.py:129
  318.2 8.0 %reduce.16 = bf16[1024,512]{1,0:T(8,128)(2,1)S(1)} reduce(bf16[1024,1,512]{2,1,0:T(2,128)(2,1)} %bitcast.242, bf16[]{:T(256)} %broadcast.330), dimensions={1}, to_apply=%bitcast.170.reduce_sub_computation | reduce | bytes 2097154
  327.9 6.3 %all-to-all-start.5 = ((bf16[8,2,32768]{2,1,0:T(2,128)(2,1)}), bf16[8,2,32768]{2,1,0:T(2,128)(2,1)}, u32[]{:S(2)}, u32[]{:S(2)}) async-start(bf16[8,2,32768]{2,1,0:T(2,128)(2,1)} %reshape.599), calls=%async_computation.5 | async-start | bytes 2097152 | tf_op jit(solution)/shard_map/all_to_all | solution.py:198
  336.2 7.0 %reduce.15 = bf16[1024,512]{1,0:T(8,128)(2,1)S(1)} reduce(bf16[1024,1,512]{2,1,0:T(2,128)(2,1)S(1)} %bitcast.243, bf16[]{:T(256)} %broadcast.330), dimensions={1}, to_apply=%bitcast.172.reduce_sub_computation | reduce | bytes 2097154
  344.8 13.1 %all-to-all-done.5 = bf16[8,2,32768]{2,1,0:T(2,128)(2,1)} async-done(((bf16[8,2,32768]{2,1,0:T(2,128)(2,1)}), bf16[8,2,32768]{2,1,0:T(2,128)(2,1)}, u32[]{:S(2)}, u32[]{:S(2)}) %all-to-all-start.5) | async-done | bytes 1048608 | tf_op jit(solution)/shard_map/all_to_all | solution.py:198
  374.5 8.1 %reduce.17 = bf16[1024,512]{1,0:T(8,128)(2,1)} reduce(bf16[1024,1,512]{2,1,0:T(2,128)(2,1)S(1)} %bitcast.244, bf16[]{:T(256)} %broadcast.330), dimensions={1}, to_apply=%bitcast.174.reduce_sub_computation | reduce | bytes 2097154
  385.9 7.0 %reduce.13 = bf16[1024,512]{1,0:T(8,128)(2,1)S(1)} reduce(bf16[1024,1,512]{2,1,0:T(2,128)(2,1)S(1)} %bitcast.240, bf16[]{:T(256)} %broadcast.330), dimensions={1}, to_apply=%bitcast.166.reduce_sub_computation | reduce | bytes 2097154
  403.7 6.0 %all-to-all-start.7 = ((bf16[8,2,32768]{2,1,0:T(2,128)(2,1)}), bf16[8,2,32768]{2,1,0:T(2,128)(2,1)}, u32[]{:S(2)}, u32[]{:S(2)}) async-start(bf16[8,2,32768]{2,1,0:T(2,128)(2,1)} %reshape.603), calls=%async_computation.7 | async-start | bytes 2097152 | tf_op jit(solution)/shard_map/all_to_all | solution.py:200
  438.3 48.3 %psum.14 = f32[2,4096]{1,0:T(2,128)S(1)} all-reduce(f32[2,4096]{1,0:T(2,128)S(1)} %pad_maximum_fusion.4), channel_id=1, replica_groups=mesh['dp'=4,'seq'=8] {'seq'}, use_global_device_ids=true, to_apply=%region_15.16 | all-reduce | flops 8192 | bytes 65536 | tf_op jit(solution)/shard_map/psum | solution.py:218
  501.6 10.3 %psum.15 = f32[2,4096]{1,0:T(2,128)S(1)} all-reduce(f32[2,4096]{1,0:T(2,128)S(1)} %psum.14), channel_id=1, replica_groups=mesh['dp'=4,'seq'=8] {'dp'}, use_global_device_ids=true, to_apply=%region_16.17 | all-reduce | flops 8192 | bytes 65536 | tf_op jit(solution)/shard_map/psum | solution.py:218
  (237 shorter events, 229.9 us)
Async XLA Ops:
  2.3 8.3 %copy-start.3 = (bf16[1,128,4096]{1,2,0:T(8,128)(2,1)}, bf16[1,128,4096]{1,2,0:T(8,128)(2,1)S(1)}, u32[]{:S(2)}) copy-start(bf16[1,128,4096]{1,2,0:T(8,128)(2,1)S(1)} %copy.156) | copy-start | bytes 3145732
  5.0 5.6 %copy-start.5 = (bf16[1,128,4096]{1,2,0:T(8,128)(2,1)}, bf16[1,128,4096]{1,2,0:T(8,128)(2,1)S(1)}, u32[]{:S(2)}) copy-start(bf16[1,128,4096]{1,2,0:T(8,128)(2,1)S(1)} %copy.153) | copy-start | bytes 3145732
  5.8 4.8 copy-start.31
  5.8 4.8 copy-start.33
  54.9 47.8 %all-to-all-start = ((bf16[8,2,32768]{2,1,0:T(2,128)(2,1)}), bf16[8,2,32768]{2,1,0:T(2,128)(2,1)}, u32[]{:S(2)}, u32[]{:S(2)}) async-start(bf16[8,2,32768]{2,1,0:T(2,128)(2,1)} %reshape.589), calls=%async_computation | async-start | bytes 2097152 | tf_op jit(solution)/shard_map/all_to_all | solution.py:160
  102.7 36.5 %all-to-all-start.1 = ((bf16[8,2,32768]{2,1,0:T(2,128)(2,1)}), bf16[8,2,32768]{2,1,0:T(2,128)(2,1)S(1)}, u32[]{:S(2)}, u32[]{:S(2)}) async-start(bf16[8,2,32768]{2,1,0:T(2,128)(2,1)} %reshape.591), calls=%async_computation.1 | async-start | bytes 2097152 | tf_op jit(solution)/shard_map/all_to_all | solution.py:161
  137.1 8.4 %copy-start.36 = (s32[1,6]{1,0:T(1,128)S(1)}, s32[1,6]{1,0:T(1,128)}, u32[]{:S(2)}) copy-start(s32[1,6]{1,0:T(1,128)} %param.18) | copy-start | bytes 76
  139.3 61.1 %all-to-all-start.2 = ((bf16[8,2,32768]{2,1,0:T(2,128)(2,1)}), bf16[8,2,32768]{2,1,0:T(2,128)(2,1)}, u32[]{:S(2)}, u32[]{:S(2)}) async-start(bf16[8,2,32768]{2,1,0:T(2,128)(2,1)} %reshape.593), calls=%async_computation.2 | async-start | bytes 2097152 | tf_op jit(solution)/shard_map/all_to_all | solution.py:162
  200.4 50.4 %all-to-all-start.4 = ((bf16[8,2,32768]{2,1,0:T(2,128)(2,1)}), bf16[8,2,32768]{2,1,0:T(2,128)(2,1)}, u32[]{:S(2)}, u32[]{:S(2)}) async-start(bf16[8,2,32768]{2,1,0:T(2,128)(2,1)} %reshape.597), calls=%async_computation.4 | async-start | bytes 2097152 | tf_op jit(solution)/shard_map/all_to_all | solution.py:174
  266.9 5.9 %copy-start.15 = (bf16[1024,4,128]{0,2,1:T(8,128)(2,1)S(1)}, bf16[1024,4,128]{0,2,1:T(8,128)(2,1)}, u32[]{:S(2)}) copy-start(bf16[1024,4,128]{0,2,1:T(8,128)(2,1)} %get-tuple-element.556) | copy-start | bytes 3145732 | tf_op jit(solution)/shard_map/while
  266.9 5.9 %copy-start.24 = (bf16[1024,4,128]{2,0,1:T(8,128)(2,1)S(1)}, bf16[1024,4,128]{2,0,1:T(8,128)(2,1)}, u32[]{:S(2)}) copy-start(bf16[1024,4,128]{2,0,1:T(8,128)(2,1)} %get-tuple-element.557) | copy-start | bytes 3145732 | tf_op jit(solution)/shard_map/while
  277.9 6.2 %copy-start.2 = (f32[4,512,1024]{2,1,0:T(8,128)S(1)}, f32[4,512,1024]{2,1,0:T(8,128)}, u32[]{:S(2)}) copy-start(f32[4,512,1024]{2,1,0:T(8,128)} %copy-done.1) | copy-start | bytes 25165828 | tf_op jit(solution)/shard_map/while
  289.9 5.9 %copy-start.15 = (bf16[1024,4,128]{0,2,1:T(8,128)(2,1)S(1)}, bf16[1024,4,128]{0,2,1:T(8,128)(2,1)}, u32[]{:S(2)}) copy-start(bf16[1024,4,128]{0,2,1:T(8,128)(2,1)} %get-tuple-element.556) | copy-start | bytes 3145732 | tf_op jit(solution)/shard_map/while
  289.9 5.9 %copy-start.24 = (bf16[1024,4,128]{2,0,1:T(8,128)(2,1)S(1)}, bf16[1024,4,128]{2,0,1:T(8,128)(2,1)}, u32[]{:S(2)}) copy-start(bf16[1024,4,128]{2,0,1:T(8,128)(2,1)} %get-tuple-element.557) | copy-start | bytes 3145732 | tf_op jit(solution)/shard_map/while
  300.9 6.2 %copy-start.2 = (f32[4,512,1024]{2,1,0:T(8,128)S(1)}, f32[4,512,1024]{2,1,0:T(8,128)}, u32[]{:S(2)}) copy-start(f32[4,512,1024]{2,1,0:T(8,128)} %copy-done.1) | copy-start | bytes 25165828 | tf_op jit(solution)/shard_map/while
  327.9 30.1 %all-to-all-start.5 = ((bf16[8,2,32768]{2,1,0:T(2,128)(2,1)}), bf16[8,2,32768]{2,1,0:T(2,128)(2,1)}, u32[]{:S(2)}, u32[]{:S(2)}) async-start(bf16[8,2,32768]{2,1,0:T(2,128)(2,1)} %reshape.599), calls=%async_computation.5 | async-start | bytes 2097152 | tf_op jit(solution)/shard_map/all_to_all | solution.py:198
  343.2 19.4 %copy-start.30 = (f32[4096]{0:T(1024)S(1)}, f32[4096]{0:T(1024)}, u32[]{:S(2)}) copy-start(f32[4096]{0:T(1024)} %param.16) | copy-start | bytes 49156
  343.2 19.5 %copy-start.28 = (f32[4096]{0:T(1024)S(1)}, f32[4096]{0:T(1024)}, u32[]{:S(2)}) copy-start(f32[4096]{0:T(1024)} %param.17) | copy-start | bytes 49156
  343.2 19.5 %copy-start.21 = (f32[128,128]{0,1:T(8,128)S(1)}, f32[128,128]{0,1:T(8,128)}, u32[]{:S(2)}) copy-start(f32[128,128]{0,1:T(8,128)} %copy-done.20) | copy-start | bytes 196612
  357.9 45.8 %all-to-all-start.6 = ((bf16[8,2,32768]{2,1,0:T(2,128)(2,1)}), bf16[8,2,32768]{2,1,0:T(2,128)(2,1)}, u32[]{:S(2)}, u32[]{:S(2)}) async-start(bf16[8,2,32768]{2,1,0:T(2,128)(2,1)} %reshape.601), calls=%async_computation.6 | async-start | bytes 2097152 | tf_op jit(solution)/shard_map/all_to_all | solution.py:199
  374.5 10.7 %copy-start.17 = (bf16[2,512,4,128]{3,2,1,0:T(4,128)(2,1)S(1)}, bf16[2,512,4,128]{3,2,1,0:T(4,128)(2,1)}, u32[]{:S(2)}) copy-start(bf16[2,512,4,128]{3,2,1,0:T(4,128)(2,1)} %copy.164) | copy-start | bytes 3145732
  403.7 30.2 %all-to-all-start.7 = ((bf16[8,2,32768]{2,1,0:T(2,128)(2,1)}), bf16[8,2,32768]{2,1,0:T(2,128)(2,1)}, u32[]{:S(2)}, u32[]{:S(2)}) async-start(bf16[8,2,32768]{2,1,0:T(2,128)(2,1)} %reshape.603), calls=%async_computation.7 | async-start | bytes 2097152 | tf_op jit(solution)/shard_map/all_to_all | solution.py:200
  431.5 55.0 %copy-start.4 = (bf16[1,128,4096]{1,2,0:T(8,128)(2,1)S(1)}, bf16[1,128,4096]{1,2,0:T(8,128)(2,1)}, u32[]{:S(2)}) copy-start(bf16[1,128,4096]{1,2,0:T(8,128)(2,1)} %copy-done.3) | copy-start | bytes 3145732
  434.0 78.5 %all-to-all-start.3 = ((bf16[8,2,32768]{2,1,0:T(2,128)(2,1)}), bf16[8,2,32768]{2,1,0:T(2,128)(2,1)}, u32[]{:S(2)}, u32[]{:S(2)}) async-start(bf16[8,2,32768]{2,1,0:T(2,128)(2,1)} %reshape.595), calls=%async_computation.3 | async-start | bytes 2097152 | tf_op jit(solution)/shard_map/all_to_all | solution.py:171
  (30 other events, 77.0 us)
